TPU v7x, 256 devices: a whole 4x4x8 slice. The times are simulated.
256 devices in a mesh: grp: 8 (over z_lo, core), dev: 32 (over z_hi, x, y).
Axes of the slice: x: 4, y: 4, z: 8 (z_hi: 2, z_lo: 4; z = z_hi * 4 + z_lo), core: 2. Of those that a mesh axis runs over, the one named last changes fastest.
Arguments:
- images: bfloat16 [131072, 64, 128], P(('grp', 'dev')), may hold values from -16 to 16
- test_maps: bfloat16 [64, 128, 32], replicated, may hold values from -6 to 6
- counts: int32 [64], replicated, may hold values from 24 to 64, as said below
Outputs:
- projected: bfloat16 [131072, 64, 32], P(('grp', 'dev'))
Inputs may be any that keep to these rules, and one draw needn't show every extreme that they name: `counts`: block 0 has 64 radial functions and block 63 has 24.
All inputs are finite; a program needn't handle non-finite values.
Results may differ from a plain program's by a relative error of at most 0.0049.
Values may be sent and summed in bfloat16 or wider, within the bound.
No kernel may reach another device: no remote copies, remote signals or barrier semaphores. Data moves between devices by JAX's collectives and lax.ppermute only.
A program may use at most 64 MiB of HBM per device.

v0:
```python
import jax
import jax.numpy as jnp
from jax import lax
from jax.sharding import PartitionSpec as P


def orthonormal(summed):
    gram_matrix = jnp.einsum("krs,krt->kst", summed, summed, precision=lax.Precision.HIGHEST)
    factor = jnp.linalg.cholesky(gram_matrix)
    solved = lax.linalg.triangular_solve(
        factor, summed, left_side=False, lower=True, transpose_a=True
    )
    return solved.astype(jnp.bfloat16)


def body(images, test_maps, counts):
    columns = images.shape[2]
    radial = columns // 2
    position = lax.broadcasted_iota(jnp.int32, (images.shape[1], columns), 1) % radial
    valid_mask = (position < counts[:, None]).astype(jnp.bfloat16)
    masked = images * valid_mask[None]
    sketch = jnp.einsum(
        "ikr,krs->iks", masked, test_maps, preferred_element_type=jnp.float32
    ).astype(jnp.bfloat16)
    partial_sum = jnp.einsum("ikr,iks->krs", masked, sketch, preferred_element_type=jnp.float32)
    totals = lax.psum(partial_sum, "grp")
    owned = lax.psum_scatter(totals, "dev", scatter_dimension=0, tiled=True)
    basis_all = lax.all_gather(orthonormal(owned), "dev", axis=0, tiled=True)
    projected = jnp.einsum("ikr,krs->iks", masked, basis_all, preferred_element_type=jnp.float32)
    return projected.astype(jnp.bfloat16)


def solution(mesh):
    in_specs = (P(("grp", "dev"), None, None), P(), P())
    out_specs = P(("grp", "dev"), None, None)
    return jax.shard_map(body, mesh=mesh, in_specs=in_specs, out_specs=out_specs, check_vma=False)
```

profile of v0, /device:TPU:8, one launch (start us, length us, event | category | flops | bytes accessed | tf_op | source)
XLA Modules:
  0.0 447.4 jit_solution(9453604602450856554)
XLA Ops:
  6.5 0.0 copy-start
  6.5 0.0 reduce-scatter.2.cloned.1.call-start
  6.5 0.8 fusion.16
  7.3 7.2 %broadcast_multiply_fusion = bf16[512,64,128]{2,1,0:T(8,128)(2,1)} fusion(bf16[512,64,128]{2,1,0:T(8,128)(2,1)} %param.3, bf16[64,128]{1,0:T(8,128)(2,1)S(1)} %fusion.16), kind=kLoop, calls=%fused_computation.6 | loop fusion | flops 4194304 | bytes 16793600 | tf_op jit(solution)/shard_map/mul | solution.py:21
  14.5 0.0 copy-done
  14.5 24.3 %fusion.4 = f32[64,128,32]{1,2,0:T(8,128)} fusion(bf16[512,64,128]{2,1,0:T(8,128)(2,1)} %broadcast_multiply_fusion, bf16[64,128,32]{1,2,0:T(8,128)(2,1)S(1)} %copy-done), kind=kOutput, calls=%fused_computation.4 | convolution fusion | flops 537919488 | bytes 9961472 | tf_op jit(solution)/shard_map/ikr,iks->krs/dot_general | solution.py:25
  38.8 0.0 reduce-scatter.2.cloned.1.call-update
  38.9 222.5 %reduce-scatter.2.cloned.1.call-done = f32[2,128,32]{1,2,0:T(8,128)} async-done(((f32[64,128,32]{1,2,0:T(8,128)}), f32[2,128,32]{1,2,0:T(8,128)}) %reduce-scatter.2.cloned.1.call-update) | async-done | bytes 32784 | tf_op jit(solution)/shard_map/reduce_scatter | solution.py:27
  261.4 26.5 %psum.8 = f32[2,128,32]{1,2,0:T(8,128)S(1)} all-reduce(f32[2,128,32]{1,2,0:T(8,128)} %reduce-scatter.2.cloned.1.call-done), channel_id=1, replica_groups=mesh['grp'=8,'dev'=32] {'grp'}, use_global_device_ids=true, to_apply=%region_0.1 | all-reduce | flops 8192 | bytes 65536 | tf_op jit(solution)/shard_map/psum | solution.py:26
  287.9 0.2 fusion.17
  288.1 0.1 copy.12
  288.2 5.9 %custom-call.7 = f32[2,32,32]{2,1,0:T(8,128)S(1)} custom-call(f32[2,32,32]{2,1,0:T(8,128)S(1)} %fusion.15), custom_call_target="Cholesky" | custom-call | tf_op jit(solution)/shard_map/jit(cholesky)/cholesky | solution.py:9
  294.1 0.1 compare_reduce_fusion
  294.2 0.1 select_bitcast_fusion
  294.3 4.9 %custom-call.8 = f32[2,1,32,32]{2,3,1,0:T(8,128)S(1)} custom-call(f32[2,1,32,32]{3,2,1,0:T(8,128)S(1)} %select_bitcast_fusion), custom_call_target="InvertDiagBlocksLowerTriangular" | custom-call | tf_op jit(solution)/shard_map/triangular_solve | solution.py:10
  299.2 0.3 convolution_convert_fusion
  299.4 119.3 %all_gather.3 = bf16[64,128,32]{1,2,0:T(8,128)(2,1)S(1)} all-gather(bf16[2,128,32]{1,2,0:T(8,128)(2,1)S(1)} %convolution_convert_fusion), channel_id=1, replica_groups=mesh['grp'=8,'dev'=32] {'dev'}, dimensions={0}, use_global_device_ids=true | all-gather | bytes 540672 | tf_op jit(solution)/shard_map/all_gather | solution.py:28
  418.8 21.8 %convert_bitcast_fusion = bf16[512,64,32]{0,2,1:T(8,128)(2,1)} fusion(bf16[64,128,32]{1,2,0:T(8,128)(2,1)S(1)} %all_gather.3, bf16[512,64,128]{2,1,0:T(8,128)(2,1)} %broadcast_multiply_fusion), kind=kOutput, calls=%fused_computation.8 | convolution fusion | flops 269484032 | bytes 11010048 | tf_op jit(solution)/shard_map/ikr,krs->iks/dot_general | solution.py:29
  (6 shorter events, 0.1 us)
Async XLA Ops:
  6.5 8.0 %copy-start = (bf16[64,128,32]{1,2,0:T(8,128)(2,1)S(1)}, bf16[64,128,32]{1,2,0:T(8,128)(2,1)}, u32[]{:S(2)}) copy-start(bf16[64,128,32]{1,2,0:T(8,128)(2,1)} %param.4) | copy-start | bytes 1572868
  6.5 254.9 %reduce-scatter.2.cloned.1.call-start = ((), (), s32[]{:S(2)}) async-start(), calls=%async_computation.1 | async-start | bytes 1081344 | tf_op jit(solution)/shard_map/reduce_scatter | solution.py:27
Sparse Core Ops, SparseCore 0:
  39.0 222.4 reduce-scatter.1
where the time goes:
time: 448 us; the launch traced here: 447 us
  waiting for transfers between devices  223 us (50%)
  blocking collectives  146 us (33%)
  matrix products  46.5 us (10%)
  other arithmetic  19 us (4%)
  between operations  13.4 us (3%)
    reduce_scatter x1, waiting for transfers between devices, body(): owned = lax.psum_scatter(totals, 'dev', scatter_dimension=0, tiled=True)  223 us
    all_gather x1, blocking collectives, body(): basis_all = lax.all_gather(orthonormal(owned), 'dev', axis=0, tiled=True)  119 us
    psum x1, blocking collectives, body(): totals = lax.psum(partial_sum, 'grp')  26.5 us
    dot_general x1, matrix products, body(): jnp.einsum('ikr,iks->krs', masked, sketch, preferred_element_type=jnp.flo...  24.3 us
    dot_general x1, matrix products, body(): jnp.einsum('ikr,krs->iks', masked, basis_all, preferred_element_type=jnp....  21.8 us
  transfers between devices with their start and end apart: 1, of which 1 were waited for; matrix products, arithmetic and copies ran while one was open for 0% of the time, Pallas kernels for 0%

commit v1 on v0

v1 whole, which is shorter than its diff:
```python
import jax
import jax.numpy as jnp
from jax import lax
from jax.sharding import Mesh, PartitionSpec as P

AXES = ("zl", "co", "zh", "x", "y")
F32, BF16 = jnp.float32, jnp.bfloat16


def orthonormal(summed_t):
    gram_matrix = jnp.einsum("ksr,ktr->kst", summed_t, summed_t, precision=lax.Precision.HIGHEST)
    factor = jnp.linalg.cholesky(gram_matrix)
    solved = lax.linalg.triangular_solve(factor, summed_t, left_side=True, lower=True)
    return solved.astype(BF16)


def body(images, test_maps, counts):
    blocks, columns = images.shape[1], images.shape[2]
    rank = test_maps.shape[2]
    radial = columns // 2
    half, own = blocks // 2, blocks // 32
    core = lax.axis_index("co")
    place = lax.axis_index("x") * 4 + lax.axis_index("y")
    position = lax.broadcasted_iota(jnp.int32, (blocks, columns), 1) % radial
    valid = position < counts[:, None]
    maps_t = jnp.where(valid[:, None, :], jnp.swapaxes(test_maps, 1, 2), 0)
    sketch = jnp.einsum("ikr,ksr->iks", images, maps_t, preferred_element_type=F32).astype(BF16)
    partial = jnp.einsum("iks,ikr->ksr", sketch, images, preferred_element_type=F32)
    swap = [(0, 1), (1, 0)]
    away = lax.dynamic_slice_in_dim(partial, (1 - core) * half, half, 0).astype(BF16)
    kept = lax.dynamic_slice_in_dim(partial, core * half, half, 0)
    pair = (kept + lax.ppermute(away, "co", swap).astype(F32)).astype(BF16)
    parts = lax.all_to_all(pair, ("x", "y"), 0, 0, tiled=True)
    plane = jnp.sum(parts.reshape(16, own, rank, columns).astype(F32), 0).astype(BF16)
    copies = jnp.broadcast_to(plane[None], (8,) + plane.shape)
    parts = lax.all_to_all(copies, ("zl", "zh"), 0, 0, tiled=True)
    total = jnp.sum(parts.astype(F32), 0)
    start = core * half + place * own
    mine = lax.dynamic_slice_in_dim(valid, start, own, 0)
    basis_t = orthonormal(jnp.where(mine[:, None, :], total, 0))
    copies = jnp.broadcast_to(basis_t[None], (16,) + basis_t.shape)
    near = lax.all_to_all(copies, ("x", "y"), 0, 0, tiled=True).reshape(half, rank, columns)
    far = lax.ppermute(near, "co", swap)
    first = core == 0
    bases_t = jnp.concatenate([jnp.where(first, near, far), jnp.where(first, far, near)])
    return jnp.einsum("ikr,ksr->iks", images, bases_t, preferred_element_type=F32).astype(BF16)


def solution(mesh):
    fine = Mesh(mesh.devices.reshape(4, 2, 2, 4, 4), AXES)
    in_specs = (P(AXES, None, None), P(), P())
    out_specs = P(AXES, None, None)
    return jax.shard_map(body, mesh=fine, in_specs=in_specs, out_specs=out_specs, check_vma=False)
```

time: 448 us -> 106 us (0.24)
  the two profiles are of different devices: /device:TPU:8 before, /device:TPU:1 now
where the time goes in v1:
time: 106 us
  matrix products  43.8 us (41%)
  starting transfers between devices  20.8 us (20%)
  waiting for transfers between devices  16.6 us (16%)
  other arithmetic  12.7 us (12%)
  blocking collectives  10.8 us (10%)
    dot_general x1, matrix products, body(): jnp.einsum('ikr,ksr->iks', images, bases_t, preferred_element_type=F32)  21.8 us
    dot_general x1, matrix products, body(): jnp.einsum('iks,ikr->ksr', sketch, images, preferred_element_type=F32)  21.6 us
    all_to_all x1, blocking collectives, body(): lax.all_to_all(copies, ('x', 'y'), 0, 0, tiled=True)  10.8 us
    all_to_all x1, starting transfers between devices, body(): parts = lax.all_to_all(copies, ('zl', 'zh'), 0, 0, tiled=True)  8.19 us
    all_to_all x1, waiting for transfers between devices, body(): parts = lax.all_to_all(pair, ('x', 'y'), 0, 0, tiled=True)  7.55 us
    all_to_all x1, waiting for transfers between devices, body(): parts = lax.all_to_all(copies, ('zl', 'zh'), 0, 0, tiled=True)  6.76 us
    another operation x4, other arithmetic, orthonormal(): factor = jnp.linalg.cholesky(gram_matrix)  6.03 us
    all_to_all x1, starting transfers between devices, body(): parts = lax.all_to_all(pair, ('x', 'y'), 0, 0, tiled=True)  5.05 us
  transfers between devices with their start and end apart: 4, of which 4 were waited for; matrix products, arithmetic and copies ran while one was open for 0% of the time, Pallas kernels for 0%

profile of v1, /device:TPU:1, one launch (start us, length us, event | category | flops | bytes accessed | tf_op | source)
XLA Modules:
  0.0 105.8 jit_solution(4501351303346747208)
XLA Ops:
  0.0 0.7 select_compare_fusion
  0.8 21.6 %fusion.4 = f32[64,32,128]{2,1,0:T(8,128)S(1)} fusion(bf16[512,64,128]{2,1,0:T(8,128)(2,1)} %param.3, bf16[64,128,32]{1,2,0:T(8,128)(2,1)} %param.4, pred[64,128]{1,0:T(8,128)(4,1)S(1)} %select_compare_fusion), kind=kOutput, calls=%fused_computation.4 | convolution fusion | flops 538181632 | bytes 9969664 | tf_op jit(solution)/shard_map/iks,ikr->ksr/dot_general | solution.py:28
  22.4 3.3 %collective-permute-start = (bf16[32,32,128]{2,1,0:T(8,128)(2,1)S(1)}, bf16[32,32,128]{2,1,0:T(8,128)(2,1)S(1)}, u32[]{:S(2)}, u32[]{:S(2)}) collective-permute-start(bf16[32,32,128]{2,1,0:T(8,128)(2,1)S(1)} %dynamic-slice_convert_fusion), channel_id=1, source_target_pairs={{0,32},{32,0},{1,33},{33,1},{2,34},{34,2},{3,35},{35,3},{4,36},{36... | collective-permute-start | bytes 786440 | tf_op jit(solution)/shard_map/ppermute | solution.py:32
  25.7 1.2 %collective-permute-done = bf16[32,32,128]{2,1,0:T(8,128)(2,1)S(1)} collective-permute-done((bf16[32,32,128]{2,1,0:T(8,128)(2,1)S(1)}, bf16[32,32,128]{2,1,0:T(8,128)(2,1)S(1)}, u32[]{:S(2)}, u32[]{:S(2)}) %collective-permute-start) | collective-permute-done | bytes 262176 | tf_op jit(solution)/shard_map/ppermute | solution.py:32
  26.8 0.8 add_convert_fusion
  27.6 5.1 %all-to-all-start = ((bf16[32,32,128]{2,1,0:T(8,128)(2,1)}), bf16[32,32,128]{2,1,0:T(8,128)(2,1)S(1)}, u32[]{:S(2)}, u32[]{:S(2)}) async-start(bf16[32,32,128]{2,1,0:T(8,128)(2,1)} %add_convert_fusion), calls=%async_computation | async-start | bytes 524288 | tf_op jit(solution)/shard_map/all_to_all | solution.py:33
  32.7 7.6 %all-to-all-done = bf16[32,32,128]{2,1,0:T(8,128)(2,1)S(1)} async-done(((bf16[32,32,128]{2,1,0:T(8,128)(2,1)}), bf16[32,32,128]{2,1,0:T(8,128)(2,1)S(1)}, u32[]{:S(2)}, u32[]{:S(2)}) %all-to-all-start) | async-done | bytes 262176 | tf_op jit(solution)/shard_map/all_to_all | solution.py:33
  40.3 0.7 broadcast_in_dim.46
  40.9 8.2 %all-to-all-start.1 = ((bf16[8,2,32,128]{3,2,1,0:T(8,128)(2,1)}), bf16[8,2,32,128]{3,2,1,0:T(8,128)(2,1)S(1)}, u32[]{:S(2)}, u32[]{:S(2)}) async-start(bf16[8,2,32,128]{3,2,1,0:T(8,128)(2,1)} %broadcast_in_dim.46), calls=%async_computation.1 | async-start | bytes 262144 | tf_op jit(solution)/shard_map/all_to_all | solution.py:36
  49.2 6.8 %all-to-all-done.1 = bf16[8,2,32,128]{3,2,1,0:T(8,128)(2,1)S(1)} async-done(((bf16[8,2,32,128]{3,2,1,0:T(8,128)(2,1)}), bf16[8,2,32,128]{3,2,1,0:T(8,128)(2,1)S(1)}, u32[]{:S(2)}, u32[]{:S(2)}) %all-to-all-start.1) | async-done | bytes 131104 | tf_op jit(solution)/shard_map/all_to_all | solution.py:36
  56.0 0.2 fusion.26
  56.1 0.1 copy.9
  56.2 5.9 %custom-call.7 = f32[2,32,32]{2,1,0:T(8,128)S(1)} custom-call(f32[2,32,32]{2,1,0:T(8,128)S(1)} %fusion.24), custom_call_target="Cholesky" | custom-call | tf_op jit(solution)/shard_map/jit(cholesky)/cholesky | solution.py:12
  62.1 0.1 compare_reduce_fusion
  62.2 0.1 select_bitcast_fusion
  62.3 4.9 %custom-call.8 = f32[2,1,32,32]{2,3,1,0:T(8,128)S(1)} custom-call(f32[2,1,32,32]{3,2,1,0:T(8,128)S(1)} %select_bitcast_fusion), custom_call_target="InvertDiagBlocksLowerTriangular" | custom-call | tf_op jit(solution)/shard_map/triangular_solve | solution.py:13
  67.2 0.3 convolution_convert_fusion
  67.6 10.8 %all_to_all.15 = bf16[16,2,32,128]{3,2,1,0:T(8,128)(2,1)S(1)} all-to-all(bf16[16,2,32,128]{3,2,1,0:T(8,128)(2,1)S(1)} %broadcast_in_dim.48), channel_id=1, replica_groups=mesh['zl'=4,'co'=2,'zh'=2,'x'=4,'y'=4] {'x','y'}, dimensions={0} | all-to-all | bytes 524288 | tf_op jit(solution)/shard_map/all_to_all | solution.py:42
  78.4 4.3 %collective-permute-start.1 = (bf16[32,32,128]{2,1,0:T(8,128)(2,1)S(1)}, bf16[32,32,128]{2,1,0:T(8,128)(2,1)S(1)}, u32[]{:S(2)}, u32[]{:S(2)}) collective-permute-start(bf16[32,32,128]{2,1,0:T(8,128)(2,1)S(1)} %bitcast.19), channel_id=1, source_target_pairs={{0,32},{32,0},{1,33},{33,1},{2,34},{34,2},{3,35},{35,3},{4,36},{36... | collective-permute-start | bytes 786440 | tf_op jit(solution)/shard_map/ppermute | solution.py:43
  82.7 1.2 %collective-permute-done.1 = bf16[32,32,128]{2,1,0:T(8,128)(2,1)S(1)} collective-permute-done((bf16[32,32,128]{2,1,0:T(8,128)(2,1)S(1)}, bf16[32,32,128]{2,1,0:T(8,128)(2,1)S(1)}, u32[]{:S(2)}, u32[]{:S(2)}) %collective-permute-start.1) | collective-permute-done | bytes 262176 | tf_op jit(solution)/shard_map/ppermute | solution.py:43
  83.9 0.1 broadcast_select_fusion.1
  83.9 21.8 %convert_bitcast_fusion = bf16[512,64,32]{0,2,1:T(8,128)(2,1)} fusion(bf16[512,64,128]{2,1,0:T(8,128)(2,1)} %param.3, bf16[32,32,128]{2,1,0:T(8,128)(2,1)S(1)} %get-tuple-element.6, bf16[32,32,128]{2,1,0:T(8,128)(2,1)S(1)} %get-tuple-element.5), kind=kOutput, calls=%fused_computation.7 | convolution fusion | flops 269746176 | bytes 11010048 | tf_op jit(solution)/shard_map/ikr,ksr->iks/dot_general | solution.py:46
  (11 shorter events, 0.2 us)
Async XLA Ops:
  22.4 4.4 %collective-permute-start = (bf16[32,32,128]{2,1,0:T(8,128)(2,1)S(1)}, bf16[32,32,128]{2,1,0:T(8,128)(2,1)S(1)}, u32[]{:S(2)}, u32[]{:S(2)}) collective-permute-start(bf16[32,32,128]{2,1,0:T(8,128)(2,1)S(1)} %dynamic-slice_convert_fusion), channel_id=1, source_target_pairs={{0,32},{32,0},{1,33},{33,1},{2,34},{34,2},{3,35},{35,3},{4,36},{36... | collective-permute-start | bytes 786440 | tf_op jit(solution)/shard_map/ppermute | solution.py:32
  27.6 12.6 %all-to-all-start = ((bf16[32,32,128]{2,1,0:T(8,128)(2,1)}), bf16[32,32,128]{2,1,0:T(8,128)(2,1)S(1)}, u32[]{:S(2)}, u32[]{:S(2)}) async-start(bf16[32,32,128]{2,1,0:T(8,128)(2,1)} %add_convert_fusion), calls=%async_computation | async-start | bytes 524288 | tf_op jit(solution)/shard_map/all_to_all | solution.py:33
  40.9 15.0 %all-to-all-start.1 = ((bf16[8,2,32,128]{3,2,1,0:T(8,128)(2,1)}), bf16[8,2,32,128]{3,2,1,0:T(8,128)(2,1)S(1)}, u32[]{:S(2)}, u32[]{:S(2)}) async-start(bf16[8,2,32,128]{3,2,1,0:T(8,128)(2,1)} %broadcast_in_dim.46), calls=%async_computation.1 | async-start | bytes 262144 | tf_op jit(solution)/shard_map/all_to_all | solution.py:36
  78.4 5.5 %collective-permute-start.1 = (bf16[32,32,128]{2,1,0:T(8,128)(2,1)S(1)}, bf16[32,32,128]{2,1,0:T(8,128)(2,1)S(1)}, u32[]{:S(2)}, u32[]{:S(2)}) collective-permute-start(bf16[32,32,128]{2,1,0:T(8,128)(2,1)S(1)} %bitcast.19), channel_id=1, source_target_pairs={{0,32},{32,0},{1,33},{33,1},{2,34},{34,2},{3,35},{35,3},{4,36},{36... | collective-permute-start | bytes 786440 | tf_op jit(solution)/shard_map/ppermute | solution.py:43

commit v2 on v1

v2 whole, which is shorter than its diff:
```python
import functools

import jax
import jax.numpy as jnp
from jax import lax
from jax.experimental import pallas as pl
from jax.experimental.pallas import tpu as pltpu
from jax.sharding import Mesh, PartitionSpec as P

AXES = ("zl", "co", "zh", "x", "y")
F32, BF16 = jnp.float32, jnp.bfloat16
NT = (((1,), (1,)), ((), ()))
STEP = 8


def valid_lanes(count, shape):
    position = lax.broadcasted_iota(jnp.int32, shape, len(shape) - 1) % (shape[-1] // 2)
    return position < count


def diagonal(upper, lower):
    zero = jnp.zeros_like(upper)
    return jnp.concatenate(
        [jnp.concatenate([upper, zero], 1), jnp.concatenate([zero, lower], 1)], 0
    )


def side_by_side(ref, p):
    return jnp.concatenate([ref[2 * p], ref[2 * p + 1]], 1)


def sketch_kernel(info, x_ref, t_ref, away_ref, kept_ref, xo_ref, *, half_steps):
    g = pl.program_id(0)
    blocks, rank, columns = 2 * half_steps * STEP, t_ref.shape[1], t_ref.shape[2]
    group = (g + half_steps * (1 - info[blocks])) % (2 * half_steps)
    xo_ref[...] = pltpu.einshape("ikr->kir", x_ref[...])
    sums = []
    for p in range(STEP // 2):
        pair = side_by_side(xo_ref, p)
        maps = []
        for k in (2 * p, 2 * p + 1):
            valid = valid_lanes(info[group * STEP + k], (rank, columns))
            maps.append(jnp.where(valid, t_ref[k], jnp.zeros((), BF16)))
        sketch = lax.dot_general(diagonal(*maps), pair, NT, preferred_element_type=F32)
        both = jnp.dot(sketch.astype(BF16), pair, preferred_element_type=F32)
        sums += [both[:rank, :columns], both[rank:, columns:]]

    @pl.when(g < half_steps)
    def _():
        for k in range(STEP):
            away_ref[k] = sums[k].astype(BF16)

    @pl.when(g >= half_steps)
    def _():
        for k in range(STEP):
            kept_ref[k] = sums[k]


def sketch_sums(info, images, maps_t):
    count, blocks, columns = images.shape
    rank = maps_t.shape[1]
    steps = blocks // STEP
    half = steps // 2

    def group(g, info):
        return (g + half * (1 - info[blocks])) % steps

    return pl.pallas_call(
        functools.partial(sketch_kernel, half_steps=half),
        out_shape=[
            jax.ShapeDtypeStruct((blocks // 2, rank, columns), BF16),
            jax.ShapeDtypeStruct((blocks // 2, rank, columns), F32),
            jax.ShapeDtypeStruct((blocks, count, columns), BF16),
        ],
        grid_spec=pltpu.PrefetchScalarGridSpec(
            num_scalar_prefetch=1,
            grid=(steps,),
            in_specs=[
                pl.BlockSpec((count, STEP, columns), lambda g, s: (0, group(g, s), 0)),
                pl.BlockSpec((STEP, rank, columns), lambda g, s: (group(g, s), 0, 0)),
            ],
            out_specs=[
                pl.BlockSpec((STEP, rank, columns), lambda g, s: (jnp.minimum(g, half - 1), 0, 0)),
                pl.BlockSpec((STEP, rank, columns), lambda g, s: (jnp.maximum(g - half, 0), 0, 0)),
                pl.BlockSpec((STEP, count, columns), lambda g, s: (group(g, s), 0, 0)),
            ],
        ),
        compiler_params=pltpu.CompilerParams(vmem_limit_bytes=32 << 20),
        cost_estimate=pl.CostEstimate(flops=2**31, bytes_accessed=18 * 2**20, transcendentals=0),
        name="sketch_sums",
    )(info, *[pltpu.with_memory_space_constraint(a, pltpu.HBM) for a in (images, maps_t)])


def combine_kernel(parts_ref, out_ref):
    total = parts_ref[0].astype(F32)
    for i in range(1, parts_ref.shape[0]):
        total = total + parts_ref[i].astype(F32)
    rounded = total.astype(BF16)
    for c in range(out_ref.shape[0]):
        out_ref[c] = rounded


def combine(parts, copies):
    return pl.pallas_call(
        combine_kernel,
        out_shape=jax.ShapeDtypeStruct((copies,) + parts.shape[1:], BF16),
        compiler_params=pltpu.CompilerParams(vmem_limit_bytes=8 << 20),
        name="combine",
    )(parts)


def solve_kernel(info, parts_ref, out_ref):
    copies, own, rank, columns = out_ref.shape
    start = info[info.shape[0] - 1]
    state = []
    for b in range(own):
        total = parts_ref[0, b].astype(F32)
        for i in range(1, parts_ref.shape[0]):
            total = total + parts_ref[i, b].astype(F32)
        total = jnp.where(valid_lanes(info[start + b], (rank, columns)), total, 0.0)
        gram = lax.dot_general(
            total, total, NT, precision=lax.Precision.HIGHEST, preferred_element_type=F32
        )
        state.append((total, gram))
    row = lax.broadcasted_iota(jnp.int32, (rank, 1), 0)
    for j in range(rank):
        for b in range(own):
            total, gram = state[b]
            pivot = gram[j : j + 1, j : j + 1]
            factor = jnp.where(row > j, gram[:, j : j + 1] * (1.0 / pivot), 0.0)
            line = total[j : j + 1, :]
            total = jnp.where(row == j, total * lax.rsqrt(pivot), total - factor * line)
            state[b] = (total, gram - factor * gram[j : j + 1, :])
    for b in range(own):
        rounded = state[b][0].astype(BF16)
        for c in range(copies):
            out_ref[c, b] = rounded


def solve(info, parts, copies):
    return pl.pallas_call(
        solve_kernel,
        out_shape=jax.ShapeDtypeStruct((copies,) + parts.shape[1:], BF16),
        in_specs=[pl.BlockSpec(memory_space=pltpu.SMEM), pl.BlockSpec(memory_space=pltpu.VMEM)],
        out_specs=pl.BlockSpec(memory_space=pltpu.VMEM),
        compiler_params=pltpu.CompilerParams(vmem_limit_bytes=8 << 20),
        name="solve",
    )(info, parts)


def project_kernel(half, x_ref, b_ref, *rest):
    o_ref = rest[-1]
    rank = b_ref.shape[1]
    for p in range(STEP // 2):
        bases = diagonal(b_ref[2 * p], b_ref[2 * p + 1])
        out = lax.dot_general(bases, side_by_side(x_ref, p), NT, preferred_element_type=F32)
        o_ref[2 * p] = out[:rank].astype(BF16)
        o_ref[2 * p + 1] = out[rank:].astype(BF16)


def project(half, rows, bases_t, into=None):
    blocks, count, columns = rows.shape
    rank = bases_t.shape[1]
    steps = blocks // STEP // 2
    extra = [] if into is None else [into]
    return pl.pallas_call(
        project_kernel,
        out_shape=jax.ShapeDtypeStruct((blocks, rank, count), BF16),
        grid_spec=pltpu.PrefetchScalarGridSpec(
            num_scalar_prefetch=1,
            grid=(steps,),
            in_specs=[
                pl.BlockSpec((STEP, count, columns), lambda g, s: (s[0] * steps + g, 0, 0)),
                pl.BlockSpec((STEP, rank, columns), lambda g, s: (g, 0, 0)),
            ]
            + [pl.BlockSpec(memory_space=pl.ANY)] * len(extra),
            out_specs=pl.BlockSpec((STEP, rank, count), lambda g, s: (s[0] * steps + g, 0, 0)),
        ),
        input_output_aliases={3: 0} if extra else {},
        compiler_params=pltpu.CompilerParams(vmem_limit_bytes=16 << 20),
        cost_estimate=pl.CostEstimate(flops=2**28, bytes_accessed=6 * 2**20, transcendentals=0),
        name="project",
    )(half, rows, bases_t, *extra)


def body(images, test_maps, counts):
    blocks, columns = images.shape[1], images.shape[2]
    rank = test_maps.shape[2]
    half, own = blocks // 2, blocks // 32
    core = lax.axis_index("co").astype(jnp.int32)
    place = (lax.axis_index("x") * 4 + lax.axis_index("y")).astype(jnp.int32)
    start = core * half + place * own
    info = jnp.concatenate([counts, core[None], start[None]])
    swap = [(0, 1), (1, 0)]
    away, kept, rows = sketch_sums(info, images, jnp.swapaxes(test_maps, 1, 2))
    pair = (kept + lax.ppermute(away, "co", swap).astype(F32)).astype(BF16)
    parts = lax.all_to_all(pair, ("x", "y"), 0, 0, tiled=True)
    copies = combine(parts.reshape(16, own, rank, columns), 8)
    parts = lax.all_to_all(copies, ("zl", "zh"), 0, 0, tiled=True)
    copies = solve(info, parts, 16)
    near = lax.all_to_all(copies, ("x", "y"), 0, 0, tiled=True).reshape(half, rank, columns)
    far = lax.ppermute(near, "co", swap)
    out = project(core[None], rows, near)
    out = project(1 - core[None], rows, far, out)
    return jnp.transpose(out, (2, 0, 1))


def solution(mesh):
    fine = Mesh(mesh.devices.reshape(4, 2, 2, 4, 4), AXES)
    in_specs = (P(AXES, None, None), P(), P())
    out_specs = P(AXES, None, None)
    return jax.shard_map(body, mesh=fine, in_specs=in_specs, out_specs=out_specs, check_vma=False)
```

time: 106 us -> 67.6 us (0.64)
  matrix products: 43.8 us -> 0 us
  blocking collectives: 10.8 us -> 38 us
  Pallas kernels: 0 us -> 19.6 us
  waiting for transfers between devices: 16.6 us -> 1.16 us
  starting transfers between devices: 20.8 us -> 7.59 us
  other arithmetic: 12.7 us -> 0.79 us
    dot_general x3 -> x0, matrix products: 43.6 us -> none  [the longest x1 21.8 us: body(): jnp.einsum('ikr,ksr->iks', images, bases_t, preferred_element_type=F32)]
    all_to_all x0 -> x2, blocking collectives: none -> 27.2 us  [the longest x1 14.8 us: body(): parts = lax.all_to_all(copies, ('zl', 'zh'), 0, 0, tiled=True)]
    pallas_call x0 -> x5, Pallas kernels: none -> 19.6 us  [the longest x1 10.7 us: sketch_sums(): pl.pallas_call(functools.partial(sketch_kernel, half_steps=half), out_sha...]
    all_to_all x2 -> x0, waiting for transfers between devices: 14.3 us -> none  [the longest x1 7.55 us: body(): parts = lax.all_to_all(pair, ('x', 'y'), 0, 0, tiled=True)]
    all_to_all x2 -> x0, starting transfers between devices: 13.2 us -> none  [the longest x1 8.19 us: body(): parts = lax.all_to_all(copies, ('zl', 'zh'), 0, 0, tiled=True)]
    another operation x7 -> x0, other arithmetic: 11 us -> none  [the longest x4 6.03 us: orthonormal(): factor = jnp.linalg.cholesky(gram_matrix)]
    ppermute x1, waiting for transfers between devices: 1.16 us -> 0.01 us  [body(): far = lax.ppermute(near, 'co', swap)]
  transfers between devices with their start and end apart: 4 -> 2, of which waited for: 4 -> 1; matrix products, arithmetic and copies ran while one was open for 0% -> 0% of each run, Pallas kernels for 0% -> 4%
where the time goes in v2:
time: 67.6 us; the launch traced here: 67.2 us
  blocking collectives  38 us (56%)
  Pallas kernels  19.6 us (29%)
  starting transfers between devices  7.59 us (11%)
  waiting for transfers between devices  1.16 us (2%)
  other arithmetic  0.79 us (1%)
    all_to_all x1, blocking collectives, body(): parts = lax.all_to_all(copies, ('zl', 'zh'), 0, 0, tiled=True)  14.8 us
    all_to_all x1, blocking collectives, body(): parts = lax.all_to_all(pair, ('x', 'y'), 0, 0, tiled=True)  12.4 us
    all_to_all x1, blocking collectives, body(): lax.all_to_all(copies, ('x', 'y'), 0, 0, tiled=True)  10.8 us
    pallas_call x1, Pallas kernels, sketch_sums(): pl.pallas_call(functools.partial(sketch_kernel, half_steps=half), out_sha...  10.7 us
    pallas_call x2, Pallas kernels, project(): pl.pallas_call(project_kernel, out_shape=jax.ShapeDtypeStruct((blocks, ra...  5.5 us
    ppermute x1, starting transfers between devices, body(): far = lax.ppermute(near, 'co', swap)  4.3 us
    pallas_call x1, Pallas kernels, solve(): pl.pallas_call(solve_kernel, out_shape=jax.ShapeDtypeStruct((copies,) + p...  3.41 us
    ppermute x1, starting transfers between devices, body(): pair = (kept + lax.ppermute(away, 'co', swap).astype(F32)).astype(BF16)  3.29 us
  transfers between devices with their start and end apart: 2, of which 1 were waited for; matrix products, arithmetic and copies ran while one was open for 0% of the time, Pallas kernels for 4%

profile of v2, /device:TPU:1, one launch (start us, length us, event | category | flops | bytes accessed | tf_op | source)
XLA Modules:
  0.0 67.2 jit_solution(11245053221009518704)
XLA Ops:
  0.0 0.7 %pad_add_fusion.info = s32[66]{0:T(128)S(1)} fusion(s32[1]{0:T(128)} %bitcast.1, s32[1]{0:T(128)} %bitcast.half, s32[64]{0:T(128)} %param.5), kind=kLoop, calls=%fused_computation.1 | loop fusion | flops 132 | bytes 528 | tf_op jit(solution)/shard_map/concatenate | solution.py:193
  0.7 10.7 %sketch_sums.1 = (bf16[32,32,128]{2,1,0:T(8,128)(2,1)S(1)}, f32[32,32,128]{2,1,0:T(8,128)S(1)}, bf16[64,512,128]{2,1,0:T(8,128)(2,1)S(1)}) custom-call(s32[66]{0:T(128)S(1)} %pad_add_fusion.info, bf16[512,64,128]{2,1,0:T(8,128)(2,1)} %x_ref.1, bf16[64,32,128]{2,1,0:T(8,128)(2,1)} %bitcast.9), custom_call_target="tpu_custom_call" | custom-call | flops 2147483648 | bytes 18874368 | tf_op jit(solution)/shard_map/sketch_sums/pallas_call | solution.py:68
  11.4 3.3 %collective-permute-start = (bf16[32,32,128]{2,1,0:T(8,128)(2,1)S(1)}, bf16[32,32,128]{2,1,0:T(8,128)(2,1)S(1)}, u32[]{:S(2)}, u32[]{:S(2)}) collective-permute-start(bf16[32,32,128]{2,1,0:T(8,128)(2,1)S(1)} %get-tuple-element.10), channel_id=1, source_target_pairs={{0,32},{32,0},{1,33},{33,1},{2,34},{34,2},{3,35},{35,3},{4,36},{36... | collective-permute-start | bytes 786440 | tf_op jit(solution)/shard_map/ppermute | solution.py:196
  14.7 1.2 %collective-permute-done = bf16[32,32,128]{2,1,0:T(8,128)(2,1)S(1)} collective-permute-done((bf16[32,32,128]{2,1,0:T(8,128)(2,1)S(1)}, bf16[32,32,128]{2,1,0:T(8,128)(2,1)S(1)}, u32[]{:S(2)}, u32[]{:S(2)}) %collective-permute-start) | collective-permute-done | bytes 262176 | tf_op jit(solution)/shard_map/ppermute | solution.py:196
  15.9 0.1 add_convert_fusion
  15.9 12.4 %all_to_all.15 = bf16[32,32,128]{2,1,0:T(8,128)(2,1)S(1)} all-to-all(bf16[32,32,128]{2,1,0:T(8,128)(2,1)S(1)} %add_convert_fusion), channel_id=1, replica_groups=mesh['zl'=4,'co'=2,'zh'=2,'x'=4,'y'=4] {'x','y'}, dimensions={0} | all-to-all | bytes 524288 | tf_op jit(solution)/shard_map/all_to_all | solution.py:197
  28.4 14.8 %all_to_all.16.parts_ref = bf16[8,2,32,128]{3,2,1,0:T(8,128)(2,1)S(1)} all-to-all(bf16[8,2,32,128]{3,2,1,0:T(8,128)(2,1)S(1)} %combine.1), channel_id=1, replica_groups=mesh['zl'=4,'co'=2,'zh'=2,'x'=4,'y'=4] {'zl','zh'}, dimensions={0} | all-to-all | bytes 262144 | tf_op jit(solution)/shard_map/all_to_all | solution.py:199
  43.2 3.4 %solve.1 = bf16[16,2,32,128]{3,2,1,0:T(8,128)(2,1)S(1)} custom-call(s32[66]{0:T(128)S(1)} %pad_add_fusion.info, bf16[8,2,32,128]{3,2,1,0:T(8,128)(2,1)S(1)} %all_to_all.16.parts_ref), custom_call_target="tpu_custom_call" | custom-call | tf_op jit(solution)/shard_map/solve/pallas_call | solution.py:141
  46.6 10.8 %all_to_all.17 = bf16[16,2,32,128]{3,2,1,0:T(8,128)(2,1)S(1)} all-to-all(bf16[16,2,32,128]{3,2,1,0:T(8,128)(2,1)S(1)} %solve.1), channel_id=1, replica_groups=mesh['zl'=4,'co'=2,'zh'=2,'x'=4,'y'=4] {'x','y'}, dimensions={0} | all-to-all | bytes 524288 | tf_op jit(solution)/shard_map/all_to_all | solution.py:201
  57.4 4.3 %collective-permute-start.1 = (bf16[32,32,128]{2,1,0:T(8,128)(2,1)S(1)}, bf16[32,32,128]{2,1,0:T(8,128)(2,1)S(1)}, u32[]{:S(2)}, u32[]{:S(2)}) collective-permute-start(bf16[32,32,128]{2,1,0:T(8,128)(2,1)S(1)} %bitcast.6), channel_id=1, source_target_pairs={{0,32},{32,0},{1,33},{33,1},{2,34},{34,2},{3,35},{35,3},{4,36},{36... | collective-permute-start | bytes 786440 | tf_op jit(solution)/shard_map/ppermute | solution.py:202
  61.7 2.7 %project.2.rest_0_ = bf16[64,32,512]{2,1,0:T(8,128)(2,1)} custom-call(s32[1]{0:T(128)} %bitcast.half, bf16[64,512,128]{2,1,0:T(8,128)(2,1)S(1)} %get-tuple-element.8.x_ref, bf16[32,32,128]{2,1,0:T(8,128)(2,1)S(1)} %bitcast.7), custom_call_target="tpu_custom_call" | custom-call | flops 268435456 | bytes 6291456 | tf_op jit(solution)/shard_map/project/pallas_call | solution.py:166
  64.5 0.0 collective-permute-done.1.b_ref
  64.5 2.7 %project.3 = bf16[64,32,512]{2,1,0:T(8,128)(2,1)} custom-call(s32[1]{0:T(128)S(6)} %sub.3.half, bf16[64,512,128]{2,1,0:T(8,128)(2,1)S(1)} %get-tuple-element.8.x_ref, bf16[32,32,128]{2,1,0:T(8,128)(2,1)S(1)} %collective-permute-done.1.b_ref, bf16[64,32,512]{2,1,0:T(8,128)(2,1)} %project.2.rest_0_), custom_call_target="tpu_custom_call", output_to_operand_aliasing={{}: (3, {})} | custom-call | flops 268435456 | bytes 6291456 | tf_op jit(solution)/shard_map/project/pallas_call | solution.py:166
  (1 shorter events, 0.0 us)
Async XLA Ops:
  11.4 4.4 %collective-permute-start = (bf16[32,32,128]{2,1,0:T(8,128)(2,1)S(1)}, bf16[32,32,128]{2,1,0:T(8,128)(2,1)S(1)}, u32[]{:S(2)}, u32[]{:S(2)}) collective-permute-start(bf16[32,32,128]{2,1,0:T(8,128)(2,1)S(1)} %get-tuple-element.10), channel_id=1, source_target_pairs={{0,32},{32,0},{1,33},{33,1},{2,34},{34,2},{3,35},{35,3},{4,36},{36... | collective-permute-start | bytes 786440 | tf_op jit(solution)/shard_map/ppermute | solution.py:196
  57.4 7.1 %collective-permute-start.1 = (bf16[32,32,128]{2,1,0:T(8,128)(2,1)S(1)}, bf16[32,32,128]{2,1,0:T(8,128)(2,1)S(1)}, u32[]{:S(2)}, u32[]{:S(2)}) collective-permute-start(bf16[32,32,128]{2,1,0:T(8,128)(2,1)S(1)} %bitcast.6), channel_id=1, source_target_pairs={{0,32},{32,0},{1,33},{33,1},{2,34},{34,2},{3,35},{35,3},{4,36},{36... | collective-permute-start | bytes 786440 | tf_op jit(solution)/shard_map/ppermute | solution.py:202

commit v3 on v1

v3 whole, which is shorter than its diff:
```python
import functools

import jax
import jax.numpy as jnp
from jax import lax
from jax.experimental import pallas as pl
from jax.experimental.pallas import tpu as pltpu
from jax.sharding import Mesh, PartitionSpec as P

AXES = ("zl", "co", "zh", "x", "y")
F32, BF16 = jnp.float32, jnp.bfloat16
NT = (((1,), (1,)), ((), ()))
STEP = 8
PANEL = 4


def valid_lanes(count, shape):
    position = lax.broadcasted_iota(jnp.int32, shape, len(shape) - 1) % (shape[-1] // 2)
    return position < count


def diagonal(upper, lower):
    zero = jnp.zeros_like(upper)
    return jnp.concatenate(
        [jnp.concatenate([upper, zero], 1), jnp.concatenate([zero, lower], 1)], 0
    )


def side_by_side(ref, k):
    return jnp.concatenate([ref[k], ref[k + 1]], 1)


def sketch_kernel(counts, images, maps, *refs, half, ahead):
    first = half == "away"
    if first:
        sums_ref, rows_ref, next_ref, count_buf, map_buf, image_buf, sems = refs
    else:
        ready_ref, sums_ref, rows_ref, count_buf, map_buf, image_buf, sems = refs
    halfblocks, rank, columns = sums_ref.shape
    steps = halfblocks // STEP
    core = lax.axis_index("co")
    base = ((1 - core) if first else core) * halfblocks
    other = core * halfblocks

    def images_at(block, target, sem):
        place = pl.multiple_of(block, STEP)
        return pltpu.make_async_copy(images.at[:, pl.ds(place, STEP), :], target, sem)

    copies = []
    if first:
        copies += [images_at(base + g * STEP, image_buf.at[g], sems.at[g]) for g in range(steps)]
        copies += [
            images_at(other + g * STEP, next_ref.at[g], sems.at[steps + g]) for g in range(ahead)
        ]
    else:
        copies += [None] * ahead
        copies += [
            images_at(base + g * STEP, image_buf.at[g - ahead], sems.at[g])
            for g in range(ahead, steps)
        ]
    count_copy = pltpu.make_async_copy(counts, count_buf, sems.at[steps + ahead])
    start = pl.multiple_of(base, STEP)
    map_copy = pltpu.make_async_copy(
        maps.at[pl.ds(start, halfblocks)], map_buf, sems.at[steps + ahead + 1]
    )
    waiting = [copy for copy in copies if copy is not None]
    waiting.pop(0).start()
    count_copy.start()
    map_copy.start()
    waiting.pop(0).start()
    for g in range(steps):
        if copies[g] is None:
            source = ready_ref.at[g]
        else:
            copies[g].wait()
            source = image_buf.at[g if first else g - ahead]
        if waiting:
            waiting.pop(0).start()
        if g == 0:
            count_copy.wait()
            map_copy.wait()
        rows_ref[g * STEP : (g + 1) * STEP] = pltpu.einshape("ikr->kir", source[...])
        for k in range(g * STEP, (g + 1) * STEP, 2):
            pair = side_by_side(rows_ref, k)
            held = []
            for b in (k, k + 1):
                valid = valid_lanes(count_buf[base + b], (rank, columns))
                held.append(jnp.where(valid, map_buf[b], jnp.zeros((), BF16)))
            sketch = lax.dot_general(diagonal(*held), pair, NT, preferred_element_type=F32)
            both = jnp.dot(sketch.astype(BF16), pair, preferred_element_type=F32)
            sums_ref[k] = both[:rank, :columns].astype(sums_ref.dtype)
            sums_ref[k + 1] = both[rank:, columns:].astype(sums_ref.dtype)
    for copy in waiting:
        copy.start()
    if first:
        for copy in copies[steps:]:
            copy.wait()


def sketch_sums(half, counts, images, maps_t, ready=None):
    count, blocks, columns = images.shape
    rank = maps_t.shape[1]
    halfblocks = blocks // 2
    steps = halfblocks // STEP
    ahead = 2
    first = half == "away"
    in_hbm, in_vmem = (pl.BlockSpec(memory_space=m) for m in (pltpu.HBM, pltpu.VMEM))
    out_shape = [
        jax.ShapeDtypeStruct((halfblocks, rank, columns), BF16 if first else F32),
        jax.ShapeDtypeStruct((halfblocks, count, columns), BF16),
    ]
    if first:
        out_shape.append(jax.ShapeDtypeStruct((ahead, count, STEP, columns), BF16))
    extra = [] if first else [ready]
    buffers = steps if first else steps - ahead
    return pl.pallas_call(
        functools.partial(sketch_kernel, half=half, ahead=ahead),
        out_shape=out_shape,
        in_specs=[in_hbm] * 3 + [in_vmem] * len(extra),
        out_specs=[in_vmem] * len(out_shape),
        scratch_shapes=[
            pltpu.SMEM((blocks,), jnp.int32),
            pltpu.VMEM((halfblocks, rank, columns), BF16),
            pltpu.VMEM((buffers, count, STEP, columns), BF16),
            pltpu.SemaphoreType.DMA((steps + ahead + 2,)),
        ],
        compiler_params=pltpu.CompilerParams(vmem_limit_bytes=24 << 20),
        cost_estimate=pl.CostEstimate(flops=2**31, bytes_accessed=6 * 2**20, transcendentals=0),
        name="sketch_" + half,
    )(counts, images, maps_t, *extra)


def combine_kernel(parts_ref, out_ref):
    total = parts_ref[0].astype(F32)
    for i in range(1, parts_ref.shape[0]):
        total = total + parts_ref[i].astype(F32)
    rounded = total.astype(BF16)
    for c in range(out_ref.shape[0]):
        out_ref[c] = rounded


def combine(parts, copies):
    return pl.pallas_call(
        combine_kernel,
        out_shape=jax.ShapeDtypeStruct((copies,) + parts.shape[1:], BF16),
        compiler_params=pltpu.CompilerParams(vmem_limit_bytes=8 << 20),
        name="combine",
    )(parts)


def solve_kernel(counts, parts_ref, out_ref, count_buf, sem):
    copies, own, rank, columns = out_ref.shape
    count_copy = pltpu.make_async_copy(counts, count_buf, sem)
    count_copy.start()
    place = lax.axis_index("x") * 4 + lax.axis_index("y")
    start = lax.axis_index("co") * (counts.shape[0] // 2) + place * own
    totals = []
    for b in range(own):
        total = parts_ref[0, b].astype(F32)
        for i in range(1, parts_ref.shape[0]):
            total = total + parts_ref[i, b].astype(F32)
        totals.append(total)
    count_copy.wait()
    state = []
    for b in range(own):
        total = jnp.where(valid_lanes(count_buf[start + b], (rank, columns)), totals[b], 0.0)
        gram = lax.dot_general(
            total, total, NT, precision=lax.Precision.HIGHEST, preferred_element_type=F32
        )
        state.append((total, gram, jnp.zeros((rank, columns), F32)))
    row = lax.broadcasted_iota(jnp.int32, (rank, columns), 0)
    for panel in range(0, rank, PANEL):
        for b in range(own):
            total, gram, scale = state[b]
            cols = [
                jnp.broadcast_to(gram[:, j : j + 1], (rank, columns))
                for j in range(panel, panel + PANEL)
            ]
            for t in range(PANEL):
                j = panel + t
                pivot = cols[t][j : j + 1, :]
                factor = jnp.where(row > j, cols[t] * (1.0 / pivot), 0.0)
                scale = jnp.where(row == j, lax.rsqrt(pivot), scale)
                total = total - factor * total[j : j + 1, :]
                for u in range(t + 1, PANEL):
                    cols[u] = cols[u] - factor * cols[u][j : j + 1, :]
                gram = gram - factor[:, :rank] * gram[j : j + 1, :]
            state[b] = (total, gram, scale)
    for b in range(own):
        rounded = (state[b][0] * state[b][2]).astype(BF16)
        for c in range(copies):
            out_ref[c, b] = rounded


def solve(counts, parts, copies):
    return pl.pallas_call(
        solve_kernel,
        out_shape=jax.ShapeDtypeStruct((copies,) + parts.shape[1:], BF16),
        in_specs=[pl.BlockSpec(memory_space=pltpu.HBM), pl.BlockSpec(memory_space=pltpu.VMEM)],
        out_specs=pl.BlockSpec(memory_space=pltpu.VMEM),
        scratch_shapes=[pltpu.SMEM(counts.shape, jnp.int32), pltpu.SemaphoreType.DMA],
        compiler_params=pltpu.CompilerParams(vmem_limit_bytes=8 << 20),
        name="solve",
    )(counts, parts)


def project_kernel(rows_ref, bases_ref, *refs, half):
    out_hbm, out_buf, sems = refs[-3:]
    halfblocks, rank, columns = bases_ref.shape
    core = lax.axis_index("co")
    base = (core if half == "near" else 1 - core) * halfblocks
    copies = []
    for g in range(halfblocks // STEP):
        for k in range(g * STEP, (g + 1) * STEP, 2):
            bases = diagonal(bases_ref[k], bases_ref[k + 1])
            pair = side_by_side(rows_ref, k)
            out = lax.dot_general(bases, pair, NT, preferred_element_type=F32).astype(BF16)
            out_buf[k] = out[:rank]
            out_buf[k + 1] = out[rank:]
        done = pl.ds(g * STEP, STEP)
        place = out_hbm.at[pl.ds(base + g * STEP, STEP)]
        copies.append(pltpu.make_async_copy(out_buf.at[done], place, sems.at[g]))
        copies[-1].start()
    for copy in copies:
        copy.wait()


def project(half, rows, bases_t, into=None):
    halfblocks, count, columns = rows.shape
    rank = bases_t.shape[1]
    in_hbm, in_vmem = (pl.BlockSpec(memory_space=m) for m in (pltpu.HBM, pltpu.VMEM))
    extra = [] if into is None else [into]
    return pl.pallas_call(
        functools.partial(project_kernel, half=half),
        out_shape=jax.ShapeDtypeStruct((2 * halfblocks, rank, count), BF16),
        in_specs=[in_vmem] * 2 + [in_hbm] * len(extra),
        out_specs=in_hbm,
        input_output_aliases={2: 0} if extra else {},
        scratch_shapes=[
            pltpu.VMEM((halfblocks, rank, count), BF16),
            pltpu.SemaphoreType.DMA((halfblocks // STEP,)),
        ],
        compiler_params=pltpu.CompilerParams(vmem_limit_bytes=16 << 20),
        cost_estimate=pl.CostEstimate(flops=2**28, bytes_accessed=6 * 2**20, transcendentals=0),
        name="project_" + half,
    )(rows, bases_t, *extra)


def body(images, test_maps, counts):
    blocks, columns = images.shape[1], images.shape[2]
    rank = test_maps.shape[2]
    own = blocks // 32
    swap = [(0, 1), (1, 0)]
    maps_t = jnp.swapaxes(test_maps, 1, 2)
    images, maps_t, counts = [
        pltpu.with_memory_space_constraint(a, pltpu.HBM) for a in (images, maps_t, counts)
    ]
    away, away_rows, ready = sketch_sums("away", counts, images, maps_t)
    other = lax.ppermute(away, "co", swap)
    kept, kept_rows = sketch_sums("kept", counts, images, maps_t, ready)
    pair = (kept + other.astype(F32)).astype(BF16)
    parts = lax.all_to_all(pair, ("x", "y"), 0, 0, tiled=True)
    copies = combine(parts.reshape(16, own, rank, columns), 8)
    parts = lax.all_to_all(copies, ("zl", "zh"), 0, 0, tiled=True)
    copies = solve(counts, parts, 16)
    near = lax.all_to_all(copies, ("x", "y"), 0, 0, tiled=True)
    near = near.reshape(blocks // 2, rank, columns)
    far = lax.ppermute(near, "co", swap)
    out = project("near", kept_rows, near)
    out = project("far", away_rows, far, out)
    return jnp.transpose(out, (2, 0, 1))


def solution(mesh):
    fine = Mesh(mesh.devices.reshape(4, 2, 2, 4, 4), AXES)
    in_specs = (P(AXES, None, None), P(), P())
    out_specs = P(AXES, None, None)
    return jax.shard_map(body, mesh=fine, in_specs=in_specs, out_specs=out_specs, check_vma=False)
```

time: 106 us -> 64.9 us (0.61)
  matrix products: 43.8 us -> 0 us
  blocking collectives: 10.8 us -> 38.3 us
  Pallas kernels: 0 us -> 18.6 us
  waiting for transfers between devices: 16.6 us -> 0.01 us
  starting transfers between devices: 20.8 us -> 7.53 us
  other arithmetic: 12.7 us -> 0.07 us
    dot_general x3 -> x0, matrix products: 43.6 us -> none  [the longest x1 21.8 us: body(): jnp.einsum('ikr,ksr->iks', images, bases_t, preferred_element_type=F32)]
    all_to_all x1 -> x3, blocking collectives: 10.8 us -> 38.3 us  [the longest x1 14.8 us: body(): parts = lax.all_to_all(copies, ('zl', 'zh'), 0, 0, tiled=True)]
    pallas_call x0 -> x6, Pallas kernels: none -> 18.6 us  [the longest x2 12.2 us: sketch_sums(): pl.pallas_call(functools.partial(sketch_kernel, half=half, ahead=ahead),...]
    all_to_all x2 -> x0, waiting for transfers between devices: 14.3 us -> none  [the longest x1 7.55 us: body(): parts = lax.all_to_all(pair, ('x', 'y'), 0, 0, tiled=True)]
    all_to_all x2 -> x0, starting transfers between devices: 13.2 us -> none  [the longest x1 8.19 us: body(): parts = lax.all_to_all(copies, ('zl', 'zh'), 0, 0, tiled=True)]
    another operation x7 -> x0, other arithmetic: 11 us -> none  [the longest x4 6.03 us: orthonormal(): factor = jnp.linalg.cholesky(gram_matrix)]
    ppermute x1, waiting for transfers between devices: 1.16 us -> 0.01 us  [body(): far = lax.ppermute(near, 'co', swap)]
    ppermute x1, waiting for transfers between devices: 1.16 us -> 0.01 us  [body(): other = lax.ppermute(away, 'co', swap)]
  transfers between devices with their start and end apart: 4 -> 2, of which waited for: 4 -> 0; matrix products, arithmetic and copies ran while one was open for 0% -> 0% of each run, Pallas kernels for 0% -> 12%
where the time goes in v3:
time: 64.9 us; the launch traced here: 64.6 us
  blocking collectives  38.3 us (59%)
  Pallas kernels  18.6 us (29%)
  starting transfers between devices  7.53 us (12%)
    all_to_all x1, blocking collectives, body(): parts = lax.all_to_all(copies, ('zl', 'zh'), 0, 0, tiled=True)  14.8 us
    all_to_all x1, blocking collectives, body(): parts = lax.all_to_all(pair, ('x', 'y'), 0, 0, tiled=True)  12.6 us
    pallas_call x2, Pallas kernels, sketch_sums(): pl.pallas_call(functools.partial(sketch_kernel, half=half, ahead=ahead),...  12.2 us
    all_to_all x1, blocking collectives, body(): near = lax.all_to_all(copies, ('x', 'y'), 0, 0, tiled=True)  10.9 us
    ppermute x1, starting transfers between devices, body(): far = lax.ppermute(near, 'co', swap)  4.24 us
    pallas_call x2, Pallas kernels, project(): pl.pallas_call(functools.partial(project_kernel, half=half), out_shape=ja...  4.24 us
    ppermute x1, starting transfers between devices, body(): other = lax.ppermute(away, 'co', swap)  3.29 us
    pallas_call x1, Pallas kernels, solve(): pl.pallas_call(solve_kernel, out_shape=jax.ShapeDtypeStruct((copies,) + p...  2.18 us
  transfers between devices with their start and end apart: 2, of which 0 were waited for; matrix products, arithmetic and copies ran while one was open for 0% of the time, Pallas kernels for 12%

profile of v3, /device:TPU:1, one launch (start us, length us, event | category | flops | bytes accessed | tf_op | source)
XLA Modules:
  0.0 64.6 jit_solution(4671500107306975497)
XLA Ops:
  0.0 6.7 %sketch_away.1 = (bf16[32,32,128]{2,1,0:T(8,128)(2,1)S(1)}, bf16[32,512,128]{2,1,0:T(8,128)(2,1)S(1)}, bf16[2,512,8,128]{3,2,1,0:T(8,128)(2,1)S(1)}) custom-call(s32[64]{0:T(128)} %counts.5, bf16[512,64,128]{2,1,0:T(8,128)(2,1)} %images.3, bf16[64,32,128]{2,1,0:T(8,128)(2,1)} %bitcast.7), custom_call_target="tpu_custom_call" | custom-call | flops 2147483648 | bytes 6291456 | tf_op jit(solution)/shard_map/sketch_away/pallas_call | solution.py:116
  6.7 3.3 %collective-permute-start = (bf16[32,32,128]{2,1,0:T(8,128)(2,1)S(1)}, bf16[32,32,128]{2,1,0:T(8,128)(2,1)S(1)}, u32[]{:S(2)}, u32[]{:S(2)}) collective-permute-start(bf16[32,32,128]{2,1,0:T(8,128)(2,1)S(1)} %get-tuple-element.13), channel_id=1, source_target_pairs={{0,32},{32,0},{1,33},{33,1},{2,34},{34,2},{3,35},{35,3},{4,36},{36... | collective-permute-start | bytes 786440 | tf_op jit(solution)/shard_map/ppermute | solution.py:259
  10.0 5.5 %sketch_kept.1 = (f32[32,32,128]{2,1,0:T(8,128)S(1)}, bf16[32,512,128]{2,1,0:T(8,128)(2,1)S(1)}) custom-call(s32[64]{0:T(128)} %counts.5, bf16[512,64,128]{2,1,0:T(8,128)(2,1)} %images.3, bf16[64,32,128]{2,1,0:T(8,128)(2,1)} %bitcast.8, bf16[2,512,8,128]{3,2,1,0:T(8,128)(2,1)S(1)} %get-tuple-element.11.refs_0_), custom_call_target="tpu_custom_call" | custom-call | flops 2147483648 | bytes 6291456 | tf_op jit(solution)/shard_map/sketch_kept/pallas_call | solution.py:116
  15.5 0.0 collective-permute-done
  15.5 0.1 add_convert_fusion
  15.6 12.6 %all_to_all.15 = bf16[32,32,128]{2,1,0:T(8,128)(2,1)S(1)} all-to-all(bf16[32,32,128]{2,1,0:T(8,128)(2,1)S(1)} %add_convert_fusion), channel_id=1, replica_groups=mesh['zl'=4,'co'=2,'zh'=2,'x'=4,'y'=4] {'x','y'}, dimensions={0} | all-to-all | bytes 524288 | tf_op jit(solution)/shard_map/all_to_all | solution.py:262
  28.2 14.8 %all_to_all.16.parts_ref = bf16[8,2,32,128]{3,2,1,0:T(8,128)(2,1)S(1)} all-to-all(bf16[8,2,32,128]{3,2,1,0:T(8,128)(2,1)S(1)} %combine.1), channel_id=1, replica_groups=mesh['zl'=4,'co'=2,'zh'=2,'x'=4,'y'=4] {'zl','zh'}, dimensions={0} | all-to-all | bytes 262144 | tf_op jit(solution)/shard_map/all_to_all | solution.py:264
  43.0 2.2 %solve.1 = bf16[16,2,32,128]{3,2,1,0:T(8,128)(2,1)S(1)} custom-call(s32[64]{0:T(128)} %counts.5, bf16[8,2,32,128]{3,2,1,0:T(8,128)(2,1)S(1)} %all_to_all.16.parts_ref), custom_call_target="tpu_custom_call" | custom-call | tf_op jit(solution)/shard_map/solve/pallas_call | solution.py:196
  45.2 10.9 %all_to_all.17 = bf16[16,2,32,128]{3,2,1,0:T(8,128)(2,1)S(1)} all-to-all(bf16[16,2,32,128]{3,2,1,0:T(8,128)(2,1)S(1)} %solve.1), channel_id=1, replica_groups=mesh['zl'=4,'co'=2,'zh'=2,'x'=4,'y'=4] {'x','y'}, dimensions={0} | all-to-all | bytes 524288 | tf_op jit(solution)/shard_map/all_to_all | solution.py:266
  56.1 4.2 %collective-permute-start.1 = (bf16[32,32,128]{2,1,0:T(8,128)(2,1)S(1)}, bf16[32,32,128]{2,1,0:T(8,128)(2,1)S(1)}, u32[]{:S(2)}, u32[]{:S(2)}) collective-permute-start(bf16[32,32,128]{2,1,0:T(8,128)(2,1)S(1)} %bitcast.4), channel_id=1, source_target_pairs={{0,32},{32,0},{1,33},{33,1},{2,34},{34,2},{3,35},{35,3},{4,36},{36... | collective-permute-start | bytes 786440 | tf_op jit(solution)/shard_map/ppermute | solution.py:268
  60.4 2.1 %project_near.1.refs_0_ = bf16[64,32,512]{2,1,0:T(8,128)(2,1)} custom-call(bf16[32,512,128]{2,1,0:T(8,128)(2,1)S(1)} %get-tuple-element.14.rows_ref, bf16[32,32,128]{2,1,0:T(8,128)(2,1)S(1)} %bitcast.5), custom_call_target="tpu_custom_call" | custom-call | flops 268435456 | bytes 6291456 | tf_op jit(solution)/shard_map/project_near/pallas_call | solution.py:233
  62.5 0.0 collective-permute-done.1.bases_ref
  62.5 2.1 %project_far.1 = bf16[64,32,512]{2,1,0:T(8,128)(2,1)} custom-call(bf16[32,512,128]{2,1,0:T(8,128)(2,1)S(1)} %get-tuple-element.10.rows_ref, bf16[32,32,128]{2,1,0:T(8,128)(2,1)S(1)} %collective-permute-done.1.bases_ref, bf16[64,32,512]{2,1,0:T(8,128)(2,1)} %project_near.1.refs_0_), custom_call_target="tpu_custom_call", output_to_operand_aliasing={{}: (2, {})} | custom-call | flops 268435456 | bytes 6291456 | tf_op jit(solution)/shard_map/project_far/pallas_call | solution.py:233
  (1 shorter events, 0.0 us)
Async XLA Ops:
  6.7 8.8 %collective-permute-start = (bf16[32,32,128]{2,1,0:T(8,128)(2,1)S(1)}, bf16[32,32,128]{2,1,0:T(8,128)(2,1)S(1)}, u32[]{:S(2)}, u32[]{:S(2)}) collective-permute-start(bf16[32,32,128]{2,1,0:T(8,128)(2,1)S(1)} %get-tuple-element.13), channel_id=1, source_target_pairs={{0,32},{32,0},{1,33},{33,1},{2,34},{34,2},{3,35},{35,3},{4,36},{36... | collective-permute-start | bytes 786440 | tf_op jit(solution)/shard_map/ppermute | solution.py:259
  56.1 6.4 %collective-permute-start.1 = (bf16[32,32,128]{2,1,0:T(8,128)(2,1)S(1)}, bf16[32,32,128]{2,1,0:T(8,128)(2,1)S(1)}, u32[]{:S(2)}, u32[]{:S(2)}) collective-permute-start(bf16[32,32,128]{2,1,0:T(8,128)(2,1)S(1)} %bitcast.4), channel_id=1, source_target_pairs={{0,32},{32,0},{1,33},{33,1},{2,34},{34,2},{3,35},{35,3},{4,36},{36... | collective-permute-start | bytes 786440 | tf_op jit(solution)/shard_map/ppermute | solution.py:268

commit v4 on v3

--- a/solution.py
+++ b/solution.py
@@ -30,104 +30,83 @@
     return jnp.concatenate([ref[k], ref[k + 1]], 1)
 
 
-def sketch_kernel(counts, images, maps, *refs, half, ahead):
-    first = half == "away"
-    if first:
-        sums_ref, rows_ref, next_ref, count_buf, map_buf, image_buf, sems = refs
-    else:
-        ready_ref, sums_ref, rows_ref, count_buf, map_buf, image_buf, sems = refs
-    halfblocks, rank, columns = sums_ref.shape
-    steps = halfblocks // STEP
-    core = lax.axis_index("co")
-    base = ((1 - core) if first else core) * halfblocks
-    other = core * halfblocks
-
-    def images_at(block, target, sem):
-        place = pl.multiple_of(block, STEP)
-        return pltpu.make_async_copy(images.at[:, pl.ds(place, STEP), :], target, sem)
-
-    copies = []
-    if first:
-        copies += [images_at(base + g * STEP, image_buf.at[g], sems.at[g]) for g in range(steps)]
-        copies += [
-            images_at(other + g * STEP, next_ref.at[g], sems.at[steps + g]) for g in range(ahead)
-        ]
-    else:
-        copies += [None] * ahead
-        copies += [
-            images_at(base + g * STEP, image_buf.at[g - ahead], sems.at[g])
-            for g in range(ahead, steps)
-        ]
-    count_copy = pltpu.make_async_copy(counts, count_buf, sems.at[steps + ahead])
-    start = pl.multiple_of(base, STEP)
-    map_copy = pltpu.make_async_copy(
-        maps.at[pl.ds(start, halfblocks)], map_buf, sems.at[steps + ahead + 1]
-    )
-    waiting = [copy for copy in copies if copy is not None]
-    waiting.pop(0).start()
-    count_copy.start()
-    map_copy.start()
-    waiting.pop(0).start()
-    for g in range(steps):
-        if copies[g] is None:
-            source = ready_ref.at[g]
-        else:
-            copies[g].wait()
-            source = image_buf.at[g if first else g - ahead]
-        if waiting:
-            waiting.pop(0).start()
-        if g == 0:
-            count_copy.wait()
-            map_copy.wait()
-        rows_ref[g * STEP : (g + 1) * STEP] = pltpu.einshape("ikr->kir", source[...])
-        for k in range(g * STEP, (g + 1) * STEP, 2):
-            pair = side_by_side(rows_ref, k)
-            held = []
-            for b in (k, k + 1):
-                valid = valid_lanes(count_buf[base + b], (rank, columns))
-                held.append(jnp.where(valid, map_buf[b], jnp.zeros((), BF16)))
-            sketch = lax.dot_general(diagonal(*held), pair, NT, preferred_element_type=F32)
-            both = jnp.dot(sketch.astype(BF16), pair, preferred_element_type=F32)
-            sums_ref[k] = both[:rank, :columns].astype(sums_ref.dtype)
-            sums_ref[k + 1] = both[rank:, columns:].astype(sums_ref.dtype)
-    for copy in waiting:
-        copy.start()
-    if first:
-        for copy in copies[steps:]:
-            copy.wait()
-
-
-def sketch_sums(half, counts, images, maps_t, ready=None):
+def sketch_kernel(core, x_ref, t_ref, counts, away_ref, kept_ref, xo_ref, *, half_steps):
+    g = pl.program_id(0)
+    rank, columns = t_ref.shape[1:]
+    group = (g + half_steps * (1 - core[0])) % (2 * half_steps)
+    xo_ref[...] = pltpu.einshape("ikr->kir", x_ref[...])
+    sums, sketches = [None] * STEP, [None] * (STEP // 2)
+
+    def project_maps(p):
+        maps = []
+        for k in (2 * p, 2 * p + 1):
+            valid = valid_lanes(counts[group * STEP + k], (rank, columns))
+            maps.append(jnp.where(valid, t_ref[k], jnp.zeros((), BF16)))
+        sketch = lax.dot_general(
+            diagonal(*maps), side_by_side(xo_ref, 2 * p), NT, preferred_element_type=F32
+        )
+        sketches[p] = sketch.astype(BF16)
+
+    def add_up(p):
+        pair, sketch = side_by_side(xo_ref, 2 * p), sketches[p]
+        both = jnp.dot(sketch, pair, preferred_element_type=F32)
+        sums[2 * p] = both[:rank, :columns]
+        sums[2 * p + 1] = both[rank:, columns:]
+
+    project_maps(0)
+    project_maps(1)
+    project_maps(2)
+    add_up(0)
+    project_maps(3)
+    add_up(1)
+    add_up(2)
+    add_up(3)
+
+    @pl.when(g < half_steps)
+    def _():
+        for k in range(STEP):
+            away_ref[k] = sums[k].astype(BF16)
+
+    @pl.when(g >= half_steps)
+    def _():
+        for k in range(STEP):
+            kept_ref[k] = sums[k]
+
+
+def sketch_sums(core, counts, images, maps_t):
     count, blocks, columns = images.shape
     rank = maps_t.shape[1]
-    halfblocks = blocks // 2
-    steps = halfblocks // STEP
-    ahead = 2
-    first = half == "away"
-    in_hbm, in_vmem = (pl.BlockSpec(memory_space=m) for m in (pltpu.HBM, pltpu.VMEM))
-    out_shape = [
-        jax.ShapeDtypeStruct((halfblocks, rank, columns), BF16 if first else F32),
-        jax.ShapeDtypeStruct((halfblocks, count, columns), BF16),
-    ]
-    if first:
-        out_shape.append(jax.ShapeDtypeStruct((ahead, count, STEP, columns), BF16))
-    extra = [] if first else [ready]
-    buffers = steps if first else steps - ahead
-    return pl.pallas_call(
-        functools.partial(sketch_kernel, half=half, ahead=ahead),
-        out_shape=out_shape,
-        in_specs=[in_hbm] * 3 + [in_vmem] * len(extra),
-        out_specs=[in_vmem] * len(out_shape),
-        scratch_shapes=[
-            pltpu.SMEM((blocks,), jnp.int32),
-            pltpu.VMEM((halfblocks, rank, columns), BF16),
-            pltpu.VMEM((buffers, count, STEP, columns), BF16),
-            pltpu.SemaphoreType.DMA((steps + ahead + 2,)),
+    steps = blocks // STEP
+    half = steps // 2
+
+    def group(g, core):
+        return (g + half * (1 - core[0])) % steps
+
+    return pl.pallas_call(
+        functools.partial(sketch_kernel, half_steps=half),
+        out_shape=[
+            jax.ShapeDtypeStruct((blocks // 2, rank, columns), BF16),
+            jax.ShapeDtypeStruct((blocks // 2, rank, columns), F32),
+            jax.ShapeDtypeStruct((blocks, count, columns), BF16),
         ],
-        compiler_params=pltpu.CompilerParams(vmem_limit_bytes=24 << 20),
-        cost_estimate=pl.CostEstimate(flops=2**31, bytes_accessed=6 * 2**20, transcendentals=0),
-        name="sketch_" + half,
-    )(counts, images, maps_t, *extra)
+        grid_spec=pltpu.PrefetchScalarGridSpec(
+            num_scalar_prefetch=1,
+            grid=(steps,),
+            in_specs=[
+                pl.BlockSpec((count, STEP, columns), lambda g, s: (0, group(g, s), 0)),
+                pl.BlockSpec((STEP, rank, columns), lambda g, s: (group(g, s), 0, 0)),
+                pl.BlockSpec((blocks,), lambda g, s: (0,), memory_space=pltpu.SMEM),
+            ],
+            out_specs=[
+                pl.BlockSpec((STEP, rank, columns), lambda g, s: (jnp.minimum(g, half - 1), 0, 0)),
+                pl.BlockSpec((STEP, rank, columns), lambda g, s: (jnp.maximum(g - half, 0), 0, 0)),
+                pl.BlockSpec((STEP, count, columns), lambda g, s: (group(g, s), 0, 0)),
+            ],
+        ),
+        compiler_params=pltpu.CompilerParams(vmem_limit_bytes=32 << 20),
+        cost_estimate=pl.CostEstimate(flops=2**31, bytes_accessed=18 * 2**20, transcendentals=0),
+        name="sketch_sums",
+    )(core, images, maps_t, counts)
 
 
 def combine_kernel(parts_ref, out_ref):
@@ -213,7 +192,7 @@
     for g in range(halfblocks // STEP):
         for k in range(g * STEP, (g + 1) * STEP, 2):
             bases = diagonal(bases_ref[k], bases_ref[k + 1])
-            pair = side_by_side(rows_ref, k)
+            pair = side_by_side(rows_ref, base + k)
             out = lax.dot_general(bases, pair, NT, preferred_element_type=F32).astype(BF16)
             out_buf[k] = out[:rank]
             out_buf[k + 1] = out[rank:]
@@ -226,8 +205,8 @@
 
 
 def project(half, rows, bases_t, into=None):
-    halfblocks, count, columns = rows.shape
-    rank = bases_t.shape[1]
+    count = rows.shape[1]
+    halfblocks, rank, columns = bases_t.shape
     in_hbm, in_vmem = (pl.BlockSpec(memory_space=m) for m in (pltpu.HBM, pltpu.VMEM))
     extra = [] if into is None else [into]
     return pl.pallas_call(
@@ -255,9 +234,9 @@
     images, maps_t, counts = [
         pltpu.with_memory_space_constraint(a, pltpu.HBM) for a in (images, maps_t, counts)
     ]
-    away, away_rows, ready = sketch_sums("away", counts, images, maps_t)
+    core = lax.axis_index("co").astype(jnp.int32)[None]
+    away, kept, rows = sketch_sums(core, counts, images, maps_t)
     other = lax.ppermute(away, "co", swap)
-    kept, kept_rows = sketch_sums("kept", counts, images, maps_t, ready)
     pair = (kept + other.astype(F32)).astype(BF16)
     parts = lax.all_to_all(pair, ("x", "y"), 0, 0, tiled=True)
     copies = combine(parts.reshape(16, own, rank, columns), 8)
@@ -266,8 +245,8 @@
     near = lax.all_to_all(copies, ("x", "y"), 0, 0, tiled=True)
     near = near.reshape(blocks // 2, rank, columns)
     far = lax.ppermute(near, "co", swap)
-    out = project("near", kept_rows, near)
-    out = project("far", away_rows, far, out)
+    out = project("near", rows, near)
+    out = project("far", rows, far, out)
     return jnp.transpose(out, (2, 0, 1))
 
 

time: 64.9 us -> 62.5 us (0.963)
  Pallas kernels: 18.6 us -> 15.2 us
  waiting for transfers between devices: 0.01 us -> 1.16 us
    pallas_call x2 -> x1, Pallas kernels: 12.2 us -> 8.74 us  [sketch_sums(): pl.pallas_call(functools.partial(sketch_kernel, half_steps=half), out_sha...]
    ppermute x1, waiting for transfers between devices: 0.01 us -> 1.16 us  [body(): other = lax.ppermute(away, 'co', swap)]
  transfers between devices with their start and end apart: 2 -> 2, of which waited for: 0 -> 1; matrix products, arithmetic and copies ran while one was open for 0% -> 0% of each run, Pallas kernels for 12% -> 3%
where the time goes in v4:
time: 62.5 us; the launch traced here: 62.1 us
  blocking collectives  38 us (61%)
  Pallas kernels  15.2 us (24%)
  starting transfers between devices  7.59 us (12%)
  waiting for transfers between devices  1.16 us (2%)
    all_to_all x1, blocking collectives, body(): parts = lax.all_to_all(copies, ('zl', 'zh'), 0, 0, tiled=True)  14.8 us
    all_to_all x1, blocking collectives, body(): parts = lax.all_to_all(pair, ('x', 'y'), 0, 0, tiled=True)  12.4 us
    all_to_all x1, blocking collectives, body(): near = lax.all_to_all(copies, ('x', 'y'), 0, 0, tiled=True)  10.8 us
    pallas_call x1, Pallas kernels, sketch_sums(): pl.pallas_call(functools.partial(sketch_kernel, half_steps=half), out_sha...  8.74 us
    ppermute x1, starting transfers between devices, body(): far = lax.ppermute(near, 'co', swap)  4.3 us
    pallas_call x2, Pallas kernels, project(): pl.pallas_call(functools.partial(project_kernel, half=half), out_shape=ja...  4.28 us
    ppermute x1, starting transfers between devices, body(): other = lax.ppermute(away, 'co', swap)  3.29 us
    pallas_call x1, Pallas kernels, solve(): pl.pallas_call(solve_kernel, out_shape=jax.ShapeDtypeStruct((copies,) + p...  2.17 us
  transfers between devices with their start and end apart: 2, of which 1 were waited for; matrix products, arithmetic and copies ran while one was open for 0% of the time, Pallas kernels for 3%

profile of v4, /device:TPU:1, one launch (start us, length us, event | category | flops | bytes accessed | tf_op | source)
XLA Modules:
  0.0 62.1 jit_solution(5035625795249128427)
XLA Ops:
  0.0 8.7 %sketch_sums.1 = (bf16[32,32,128]{2,1,0:T(8,128)(2,1)S(1)}, f32[32,32,128]{2,1,0:T(8,128)S(1)}, bf16[64,512,128]{2,1,0:T(8,128)(2,1)S(1)}) custom-call(s32[1]{0:T(128)} %bitcast.core, bf16[512,64,128]{2,1,0:T(8,128)(2,1)} %x_ref.1, bf16[64,32,128]{2,1,0:T(8,128)(2,1)} %bitcast.8, s32[64]{0:T(128)} %counts.3), custom_call_target="tpu_custom_call" | custom-call | flops 2147483648 | bytes 18874368 | tf_op jit(solution)/shard_map/sketch_sums/pallas_call | solution.py:85
  8.7 3.3 %collective-permute-start = (bf16[32,32,128]{2,1,0:T(8,128)(2,1)S(1)}, bf16[32,32,128]{2,1,0:T(8,128)(2,1)S(1)}, u32[]{:S(2)}, u32[]{:S(2)}) collective-permute-start(bf16[32,32,128]{2,1,0:T(8,128)(2,1)S(1)} %get-tuple-element.10), channel_id=1, source_target_pairs={{0,32},{32,0},{1,33},{33,1},{2,34},{34,2},{3,35},{35,3},{4,36},{36... | collective-permute-start | bytes 786440 | tf_op jit(solution)/shard_map/ppermute | solution.py:239
  12.0 1.2 %collective-permute-done = bf16[32,32,128]{2,1,0:T(8,128)(2,1)S(1)} collective-permute-done((bf16[32,32,128]{2,1,0:T(8,128)(2,1)S(1)}, bf16[32,32,128]{2,1,0:T(8,128)(2,1)S(1)}, u32[]{:S(2)}, u32[]{:S(2)}) %collective-permute-start) | collective-permute-done | bytes 262176 | tf_op jit(solution)/shard_map/ppermute | solution.py:239
  13.2 0.1 add_convert_fusion
  13.3 12.4 %all_to_all.15 = bf16[32,32,128]{2,1,0:T(8,128)(2,1)S(1)} all-to-all(bf16[32,32,128]{2,1,0:T(8,128)(2,1)S(1)} %add_convert_fusion), channel_id=1, replica_groups=mesh['zl'=4,'co'=2,'zh'=2,'x'=4,'y'=4] {'x','y'}, dimensions={0} | all-to-all | bytes 524288 | tf_op jit(solution)/shard_map/all_to_all | solution.py:241
  25.7 14.8 %all_to_all.16.parts_ref = bf16[8,2,32,128]{3,2,1,0:T(8,128)(2,1)S(1)} all-to-all(bf16[8,2,32,128]{3,2,1,0:T(8,128)(2,1)S(1)} %combine.1), channel_id=1, replica_groups=mesh['zl'=4,'co'=2,'zh'=2,'x'=4,'y'=4] {'zl','zh'}, dimensions={0} | all-to-all | bytes 262144 | tf_op jit(solution)/shard_map/all_to_all | solution.py:243
  40.5 2.2 %solve.1 = bf16[16,2,32,128]{3,2,1,0:T(8,128)(2,1)S(1)} custom-call(s32[64]{0:T(128)} %counts.3, bf16[8,2,32,128]{3,2,1,0:T(8,128)(2,1)S(1)} %all_to_all.16.parts_ref), custom_call_target="tpu_custom_call" | custom-call | tf_op jit(solution)/shard_map/solve/pallas_call | solution.py:175
  42.7 10.8 %all_to_all.17 = bf16[16,2,32,128]{3,2,1,0:T(8,128)(2,1)S(1)} all-to-all(bf16[16,2,32,128]{3,2,1,0:T(8,128)(2,1)S(1)} %solve.1), channel_id=1, replica_groups=mesh['zl'=4,'co'=2,'zh'=2,'x'=4,'y'=4] {'x','y'}, dimensions={0} | all-to-all | bytes 524288 | tf_op jit(solution)/shard_map/all_to_all | solution.py:245
  53.5 4.3 %collective-permute-start.1 = (bf16[32,32,128]{2,1,0:T(8,128)(2,1)S(1)}, bf16[32,32,128]{2,1,0:T(8,128)(2,1)S(1)}, u32[]{:S(2)}, u32[]{:S(2)}) collective-permute-start(bf16[32,32,128]{2,1,0:T(8,128)(2,1)S(1)} %bitcast.6), channel_id=1, source_target_pairs={{0,32},{32,0},{1,33},{33,1},{2,34},{34,2},{3,35},{35,3},{4,36},{36... | collective-permute-start | bytes 786440 | tf_op jit(solution)/shard_map/ppermute | solution.py:247
  57.8 2.1 %project_near.1.refs_0_ = bf16[64,32,512]{2,1,0:T(8,128)(2,1)} custom-call(bf16[64,512,128]{2,1,0:T(8,128)(2,1)S(1)} %get-tuple-element.8.rows_ref, bf16[32,32,128]{2,1,0:T(8,128)(2,1)S(1)} %bitcast.7), custom_call_target="tpu_custom_call" | custom-call | flops 268435456 | bytes 6291456 | tf_op jit(solution)/shard_map/project_near/pallas_call | solution.py:212
  60.0 0.0 collective-permute-done.1.bases_ref
  60.0 2.1 %project_far.1 = bf16[64,32,512]{2,1,0:T(8,128)(2,1)} custom-call(bf16[64,512,128]{2,1,0:T(8,128)(2,1)S(1)} %get-tuple-element.8.rows_ref, bf16[32,32,128]{2,1,0:T(8,128)(2,1)S(1)} %collective-permute-done.1.bases_ref, bf16[64,32,512]{2,1,0:T(8,128)(2,1)} %project_near.1.refs_0_), custom_call_target="tpu_custom_call", output_to_operand_aliasing={{}: (2, {})} | custom-call | flops 268435456 | bytes 6291456 | tf_op jit(solution)/shard_map/project_far/pallas_call | solution.py:212
  (1 shorter events, 0.0 us)
Async XLA Ops:
  8.7 4.4 %collective-permute-start = (bf16[32,32,128]{2,1,0:T(8,128)(2,1)S(1)}, bf16[32,32,128]{2,1,0:T(8,128)(2,1)S(1)}, u32[]{:S(2)}, u32[]{:S(2)}) collective-permute-start(bf16[32,32,128]{2,1,0:T(8,128)(2,1)S(1)} %get-tuple-element.10), channel_id=1, source_target_pairs={{0,32},{32,0},{1,33},{33,1},{2,34},{34,2},{3,35},{35,3},{4,36},{36... | collective-permute-start | bytes 786440 | tf_op jit(solution)/shard_map/ppermute | solution.py:239
  53.5 6.4 %collective-permute-start.1 = (bf16[32,32,128]{2,1,0:T(8,128)(2,1)S(1)}, bf16[32,32,128]{2,1,0:T(8,128)(2,1)S(1)}, u32[]{:S(2)}, u32[]{:S(2)}) collective-permute-start(bf16[32,32,128]{2,1,0:T(8,128)(2,1)S(1)} %bitcast.6), channel_id=1, source_target_pairs={{0,32},{32,0},{1,33},{33,1},{2,34},{34,2},{3,35},{35,3},{4,36},{36... | collective-permute-start | bytes 786440 | tf_op jit(solution)/shard_map/ppermute | solution.py:247
